TPU v7x, 128 devices: a whole 4x4x4 slice. The times are simulated.
128 devices in a mesh: item: 4 (over z), user: 32 (over y, x, core).
Axes of the slice: x: 4, y: 4, z: 4, core: 2. Of those that a mesh axis runs over, the one named last changes fastest.
Arguments:
- interactions: bfloat16 [65536, 16384], P('user', 'item'), may hold values from 0 to 1, as said below
- omega: float32 [16384, 256], P('item'), may hold values from -6 to 6
Outputs:
- scaled_basis: float32 [16384, 256], P('item')
Inputs may be any that keep to these rules, and one draw needn't show every extreme that they name: `interactions`: every entry is 0 or 1.
All inputs are finite; a program needn't handle non-finite values.
Results may differ from a plain program's by a relative error of at most 0.0003.
Values sent between devices are 32-bit elements; how exact they have to be, the bound alone decides.
No kernel may reach another device: no remote copies, remote signals or barrier semaphores. Data moves between devices by JAX's collectives and lax.ppermute only.
A program may use at most 128 MiB of HBM per device.

v0:
```python
import jax
import jax.numpy as jnp
from jax import lax
from jax.sharding import PartitionSpec as P

ridge = 200.0
highest = lax.Precision.HIGHEST


def gram_of(block):
    return lax.dot_general(
        block,
        block,
        (((0,), (0,)), ((), ())),
        precision=highest,
        preferred_element_type=jnp.float32,
    )


def factor(block, gram):
    lower = jnp.linalg.cholesky(gram)
    return lax.linalg.triangular_solve(lower, block, left_side=False, lower=True, transpose_a=True)


def gram_wide(block):
    return lax.psum(gram_of(block), ("item", "user"))


def local(interactions, omega):
    local_rows = jnp.dot(interactions, omega, precision=highest, preferred_element_type=jnp.float32)
    user_sketch = lax.psum(local_rows, "item")
    item_count = omega.shape[0] * lax.axis_size("item")
    factor_scale = jnp.sqrt(jnp.float32(item_count))
    own_rows = omega.shape[0] // lax.axis_size("user")
    block = lax.psum_scatter(
        lax.dot_general(
            interactions,
            user_sketch,
            (((0,), (0,)), ((), ())),
            precision=highest,
            preferred_element_type=jnp.float32,
        ),
        "user",
        scatter_dimension=0,
        tiled=True,
    )
    own_omega = lax.dynamic_slice_in_dim(omega, lax.axis_index("user") * own_rows, own_rows, 0)
    block = block + ridge * own_omega
    for sweep in range(2):
        block = factor(block, gram_wide(block))
    return lax.all_gather(factor_scale * block, "user", axis=0, tiled=True)


def solution(mesh):
    in_specs = (P("user", "item"), P("item", None))
    out_specs = P("item", None)
    return jax.shard_map(local, mesh=mesh, in_specs=in_specs, out_specs=out_specs, check_vma=False)
```

profile of v0, /device:TPU:1, one launch (start us, length us, event | category | flops | bytes accessed | tf_op | source)
XLA Modules:
  0.0 661.8 jit_solution(2004291830693291663)
XLA Ops:
  6.5 18.5 %fusion.27 = f32[2048,256]{1,0:T(8,128)} fusion(bf16[2048,4096]{1,0:T(8,128)(2,1)} %param.5, f32[4096,256]{1,0:T(8,128)} %param.6), kind=kOutput, calls=%fused_computation.63 | convolution fusion | flops 25769803776 | bytes 23068672 | tf_op jit(solution)/shard_map/dot_general | solution.py:30
  25.1 62.1 %all-reduce.5.cloned.1.call-done = f32[2048,256]{1,0:T(8,128)} async-done(((f32[2048,256]{1,0:T(8,128)}), f32[2048,256]{1,0:T(8,128)}) %all-reduce.5.cloned.1.call-update) | async-done | bytes 2097168 | tf_op jit(solution)/shard_map/psum | solution.py:31
  87.2 17.8 %convolution_bitcast_fusion = f32[4096,256]{0,1:T(8,128)} fusion(f32[2048,256]{1,0:T(8,128)} %all-reduce.5.cloned.1.call-done, bf16[2048,4096]{1,0:T(8,128)(2,1)} %param.5), kind=kOutput, calls=%fused_computation.4 | convolution fusion | flops 25769803776 | bytes 23068672 | tf_op jit(solution)/shard_map/dot_general | solution.py:36
  105.0 0.9 constant_dynamic-slice_fusion.2
  106.1 79.4 %reduce-scatter.2.cloned.1.call-done = f32[128,256]{0,1:T(8,128)} async-done(((f32[4096,256]{0,1:T(8,128)}), f32[128,256]{0,1:T(8,128)}) %reduce-scatter.2.cloned.1.call-update) | async-done | bytes 131088 | tf_op jit(solution)/shard_map/reduce_scatter | solution.py:35
  185.5 0.9 multiply_add_fusion
  186.4 1.1 fusion.28
  187.5 0.2 all-reduce.9.cloned.1.call-start
  187.8 146.7 %all-reduce.7.cloned.1.call-done = f32[256,256]{0,1:T(8,128)} async-done(((f32[256,256]{0,1:T(8,128)}), f32[256,256]{0,1:T(8,128)}) %all-reduce.7.cloned.1.call-update) | async-done | bytes 262160 | tf_op jit(solution)/shard_map/psum | solution.py:26
  334.5 1.1 copy.5
  335.6 1.0 fusion.1
  336.6 11.7 %cholesky.130 = f32[128,128]{1,0:T(8,128)S(1)} custom-call(f32[128,128]{1,0:T(8,128)S(1)} %cholesky.194), custom_call_target="Cholesky" | custom-call | tf_op jit(solution)/shard_map/jit(cholesky)/cholesky | solution.py:21
  348.3 9.8 %custom-call.13 = f32[1,128,128]{1,2,0:T(8,128)S(1)} custom-call(f32[1,128,128]{2,1,0:T(8,128)S(1)} %get-tuple-element.50), custom_call_target="InvertDiagBlocksLowerTriangular" | custom-call | tf_op jit(solution)/shard_map/jit(cholesky)/cholesky | solution.py:21
  358.4 0.3 convolution_subtract_fusion.3
  358.6 11.7 %cholesky.147 = f32[128,128]{1,0:T(8,128)S(1)} custom-call(f32[128,128]{1,0:T(8,128)S(1)} %convolution_subtract_fusion.3), custom_call_target="Cholesky" | custom-call | tf_op jit(solution)/shard_map/jit(cholesky)/cholesky | solution.py:21
  370.4 0.7 compare_reduce_fusion.2
  372.6 4.1 while.4
  372.6 0.6 fusion.45
  373.2 1.4 bitcast_dynamic-update-slice_fusion.4
  374.7 0.6 fusion.45
  375.3 1.4 bitcast_dynamic-update-slice_fusion.4
  376.7 19.7 %custom-call.14 = f32[2,128,128]{1,2,0:T(8,128)S(1)} custom-call(f32[2,128,128]{2,1,0:T(8,128)S(1)} %get-tuple-element.21), custom_call_target="InvertDiagBlocksLowerTriangular" | custom-call | tf_op jit(solution)/shard_map/triangular_solve/custom-call.0 | solution.py:22
  396.4 0.3 fusion.13
  396.7 0.2 convolution_subtract_fusion.2
  396.9 0.3 fusion.11
  397.2 1.1 fusion.2
  398.3 0.3 all-gather.2.cloned.1.call-start
  398.6 140.5 %all-reduce.9.cloned.1.call-done = f32[256,256]{0,1:T(8,128)} async-done(((f32[256,256]{0,1:T(8,128)}), f32[256,256]{0,1:T(8,128)}) %all-reduce.9.cloned.1.call-update) | async-done | bytes 262160 | tf_op jit(solution)/shard_map/psum | solution.py:26
  539.0 1.1 copy.7
  540.1 1.0 fusion
  541.1 11.7 %cholesky.164 = f32[128,128]{1,0:T(8,128)S(1)} custom-call(f32[128,128]{1,0:T(8,128)S(1)} %cholesky.197), custom_call_target="Cholesky" | custom-call | tf_op jit(solution)/shard_map/jit(cholesky)/cholesky | solution.py:21
  552.9 0.6 compare_reduce_fusion.1
  553.5 9.8 %custom-call.15 = f32[1,128,128]{1,2,0:T(8,128)S(1)} custom-call(f32[1,128,128]{2,1,0:T(8,128)S(1)} %get-tuple-element.46), custom_call_target="InvertDiagBlocksLowerTriangular" | custom-call | tf_op jit(solution)/shard_map/jit(cholesky)/cholesky | solution.py:21
  563.6 0.3 convolution_subtract_fusion.1
  563.8 11.7 %cholesky.181 = f32[128,128]{1,0:T(8,128)S(1)} custom-call(f32[128,128]{1,0:T(8,128)S(1)} %convolution_subtract_fusion.1), custom_call_target="Cholesky" | custom-call | tf_op jit(solution)/shard_map/jit(cholesky)/cholesky | solution.py:21
  575.6 0.7 compare_reduce_fusion
  577.7 4.4 while.5
  578.0 0.6 fusion.46
  578.6 1.4 bitcast_dynamic-update-slice_fusion.5
  580.0 0.6 fusion.46
  580.6 1.4 bitcast_dynamic-update-slice_fusion.5
  582.1 19.7 %custom-call.16 = f32[2,128,128]{1,2,0:T(8,128)S(1)} custom-call(f32[2,128,128]{2,1,0:T(8,128)S(1)} %get-tuple-element.22), custom_call_target="InvertDiagBlocksLowerTriangular" | custom-call | tf_op jit(solution)/shard_map/triangular_solve/custom-call.0 | solution.py:22
  601.8 0.3 fusion.8
  602.1 0.2 convolution_subtract_fusion
  602.3 0.3 fusion.6
  602.6 0.7 maximum_multiply_fusion
  603.3 46.4 %all-gather.2.cloned.1.call-done = f32[4096,256]{0,1:T(8,128)} async-done(((f32[128,256]{0,1:T(8,128)}), f32[4096,256]{0,1:T(8,128)}) %all-gather.2.cloned.1.call-update) | async-done | bytes 4194320 | tf_op jit(solution)/shard_map/all_gather | solution.py:51
  649.7 5.6 copy.8
  (29 shorter events, 1.0 us)
Async XLA Ops:
  6.5 80.7 %all-reduce.5.cloned.1.call-start = ((), (), s32[]{:S(2)}) async-start(), calls=%async_computation.1 | async-start | bytes 4194304 | tf_op jit(solution)/shard_map/psum | solution.py:31
  25.1 160.4 %reduce-scatter.2.cloned.1.call-start = ((), (), s32[]{:S(2)}) async-start(), calls=%async_computation.2 | async-start | bytes 4325376 | tf_op jit(solution)/shard_map/reduce_scatter | solution.py:35
  105.0 229.5 %all-reduce.7.cloned.1.call-start = ((), (), s32[]{:S(2)}) async-start(), calls=%async_computation.3 | async-start | bytes 524288 | tf_op jit(solution)/shard_map/psum | solution.py:26
  187.5 351.5 %all-reduce.9.cloned.1.call-start = ((), (), s32[]{:S(2)}) async-start(), calls=%async_computation.4 | async-start | bytes 524288 | tf_op jit(solution)/shard_map/psum | solution.py:26
  398.3 251.4 %all-gather.2.cloned.1.call-start = ((), (), s32[]{:S(2)}) async-start(), calls=%async_computation.5 | async-start | bytes 4325376 | tf_op jit(solution)/shard_map/all_gather | solution.py:51
Sparse Core Ops, SparseCore 0:
  25.2 61.9 all-reduce.4
  105.1 80.3 reduce-scatter.1
  190.3 144.1 all-reduce.6
  398.4 140.5 all-reduce.8
  603.4 46.2 all-gather.1
where the time goes:
time: 662 us
  waiting for transfers between devices  475 us (72%)
  other arithmetic  112 us (17%)
  matrix products  40.9 us (6%)
  local copies, waits for them, and re-layouts  17 us (3%)
  between operations  16 us (2%)
    psum x2, waiting for transfers between devices, gram_wide(): return lax.psum(gram_of(block), ('item', 'user'))  287 us
    reduce_scatter x1, waiting for transfers between devices, local(): lax.psum_scatter(lax.dot_general(interactions, user_sketch, (((0,), (0,))...  79.4 us
    another operation x13, other arithmetic, factor(): lower = jnp.linalg.cholesky(gram)  68.7 us
    psum x1, waiting for transfers between devices, local(): user_sketch = lax.psum(local_rows, 'item')  62.1 us
    all_gather x1, waiting for transfers between devices, local(): return lax.all_gather(factor_scale * block, 'user', axis=0, tiled=True)  46.4 us
    another operation x5, other arithmetic, factor(): lax.linalg.triangular_solve(lower, block, left_side=False, lower=True, tr...  39.4 us
    dot_general x1, matrix products, local(): jnp.dot(interactions, omega, precision=highest, preferred_element_type=jn...  18.5 us
    dot_general x1, matrix products, local(): lax.dot_general(interactions, user_sketch, (((0,), (0,)), ((), ())), prec...  17.8 us
  transfers between devices with their start and end apart: 5, of which 5 were waited for; matrix products, arithmetic and copies ran while one was open for 0% of the time, Pallas kernels for 0%

commit v1 on v0

--- a/solution.py
+++ b/solution.py
@@ -28,7 +28,11 @@
 
 def local(interactions, omega):
     local_rows = jnp.dot(interactions, omega, precision=highest, preferred_element_type=jnp.float32)
-    user_sketch = lax.psum(local_rows, "item")
+    user_sketch = local_rows
+    for hop in (1, 2):
+        user_sketch = user_sketch + lax.ppermute(
+            user_sketch, "item", [(dev, dev ^ hop) for dev in range(4)]
+        )
     item_count = omega.shape[0] * lax.axis_size("item")
     factor_scale = jnp.sqrt(jnp.float32(item_count))
     own_rows = omega.shape[0] // lax.axis_size("user")

time: 662 us -> 704 us (1.063); the launches traced: 662 us -> 695 us
  waiting for transfers between devices: 475 us -> 506 us
    ppermute x0 -> x2, waiting for transfers between devices: none -> 89.8 us  [local(): lax.ppermute(user_sketch, 'item', [(dev, dev ^ hop) for dev in range(4)])]
    psum x1 -> x0, waiting for transfers between devices: 62.1 us -> none  [local(): user_sketch = lax.psum(local_rows, 'item')]
  transfers between devices with their start and end apart: 5 -> 6, of which waited for: 5 -> 6; matrix products, arithmetic and copies ran while one was open for 0% -> 0% of each run, Pallas kernels for 0% -> 0%
where the time goes in v1:
time: 704 us; the launch traced here: 695 us
  waiting for transfers between devices  506 us (72%)
  other arithmetic  112 us (16%)
  matrix products  37.2 us (5%)
  local copies, waits for them, and re-layouts  17 us (2%)
  between operations  16.3 us (2%)
    psum x2, waiting for transfers between devices, gram_wide(): return lax.psum(gram_of(block), ('item', 'user'))  287 us
    ppermute x2, waiting for transfers between devices, local(): lax.ppermute(user_sketch, 'item', [(dev, dev ^ hop) for dev in range(4)])  89.8 us
    reduce_scatter x1, waiting for transfers between devices, local(): lax.psum_scatter(lax.dot_general(interactions, user_sketch, (((0,), (0,))...  82.8 us
    another operation x13, other arithmetic, factor(): lower = jnp.linalg.cholesky(gram)  68.7 us
    all_gather x1, waiting for transfers between devices, local(): return lax.all_gather(factor_scale * block, 'user', axis=0, tiled=True)  46.4 us
    another operation x5, other arithmetic, factor(): lax.linalg.triangular_solve(lower, block, left_side=False, lower=True, tr...  39.4 us
    dot_general x1, matrix products, local(): jnp.dot(interactions, omega, precision=highest, preferred_element_type=jn...  17.5 us
    dot_general x1, matrix products, local(): lax.dot_general(interactions, user_sketch, (((0,), (0,)), ((), ())), prec...  15 us
  transfers between devices with their start and end apart: 6, of which 6 were waited for; matrix products, arithmetic and copies ran while one was open for 0% of the time, Pallas kernels for 0%

profile of v1, /device:TPU:1, one launch (start us, length us, event | category | flops | bytes accessed | tf_op | source)
XLA Modules:
  0.0 695.4 jit_solution(16740009601428446785)
XLA Ops:
  6.5 17.5 %fusion.29 = f32[2048,256]{1,0:T(8,128)S(1)} fusion(bf16[2048,4096]{1,0:T(8,128)(2,1)} %param.5, f32[4096,256]{1,0:T(8,128)} %param.6), kind=kOutput, calls=%fused_computation.65 | convolution fusion | flops 25769803776 | bytes 23068672 | tf_op jit(solution)/shard_map/dot_general | solution.py:30
  24.1 2.5 collective-permute-start
  26.6 45.3 %collective-permute-done = f32[2048,256]{1,0:T(8,128)S(1)} collective-permute-done((f32[2048,256]{1,0:T(8,128)S(1)}, f32[2048,256]{1,0:T(8,128)S(1)}, u32[]{:S(2)}, u32[]{:S(2)}) %collective-permute-start) | collective-permute-done | bytes 2097184 | tf_op jit(solution)/shard_map/ppermute | solution.py:33
  72.0 0.3 add.35
  72.2 3.2 collective-permute-start.1
  75.4 44.5 %collective-permute-done.1 = f32[2048,256]{1,0:T(8,128)S(1)} collective-permute-done((f32[2048,256]{1,0:T(8,128)S(1)}, f32[2048,256]{1,0:T(8,128)S(1)}, u32[]{:S(2)}, u32[]{:S(2)}) %collective-permute-start.1) | collective-permute-done | bytes 2097184 | tf_op jit(solution)/shard_map/ppermute | solution.py:33
  119.9 15.0 %convolution_bitcast_fusion = f32[4096,256]{0,1:T(8,128)} fusion(bf16[2048,4096]{1,0:T(8,128)(2,1)S(1)} %copy-done, f32[2048,256]{1,0:T(8,128)S(1)} %add.35, f32[2048,256]{1,0:T(8,128)S(1)} %collective-permute-done.1), kind=kOutput, calls=%fused_computation.4 | convolution fusion | flops 25770328064 | bytes 25165824 | tf_op jit(solution)/shard_map/dot_general | solution.py:40
  135.0 0.9 constant_dynamic-slice_fusion.2
  136.0 82.8 %reduce-scatter.2.cloned.1.call-done = f32[128,256]{0,1:T(8,128)} async-done(((f32[4096,256]{0,1:T(8,128)}), f32[128,256]{0,1:T(8,128)}) %reduce-scatter.2.cloned.1.call-update) | async-done | bytes 131088 | tf_op jit(solution)/shard_map/reduce_scatter | solution.py:39
  218.8 0.9 multiply_add_fusion
  219.8 1.1 fusion.30
  220.9 0.5 all-reduce.6.cloned.1.call-start
  221.4 146.5 %all-reduce.4.cloned.1.call-done = f32[256,256]{0,1:T(8,128)} async-done(((f32[256,256]{0,1:T(8,128)}), f32[256,256]{0,1:T(8,128)}) %all-reduce.4.cloned.1.call-update) | async-done | bytes 262160 | tf_op jit(solution)/shard_map/psum | solution.py:26
  367.9 1.1 copy.5
  369.0 1.0 fusion.2
  370.0 11.7 %cholesky.130 = f32[128,128]{1,0:T(8,128)S(1)} custom-call(f32[128,128]{1,0:T(8,128)S(1)} %cholesky.194), custom_call_target="Cholesky" | custom-call | tf_op jit(solution)/shard_map/jit(cholesky)/cholesky | solution.py:21
  381.8 9.8 %custom-call.13 = f32[1,128,128]{1,2,0:T(8,128)S(1)} custom-call(f32[1,128,128]{2,1,0:T(8,128)S(1)} %get-tuple-element.50), custom_call_target="InvertDiagBlocksLowerTriangular" | custom-call | tf_op jit(solution)/shard_map/jit(cholesky)/cholesky | solution.py:21
  391.8 0.3 convolution_subtract_fusion.2
  392.1 11.7 %cholesky.147 = f32[128,128]{1,0:T(8,128)S(1)} custom-call(f32[128,128]{1,0:T(8,128)S(1)} %convolution_subtract_fusion.2), custom_call_target="Cholesky" | custom-call | tf_op jit(solution)/shard_map/jit(cholesky)/cholesky | solution.py:21
  403.8 0.7 compare_reduce_fusion.2
  406.0 4.1 while.4
  406.0 0.6 fusion.45
  406.6 1.4 bitcast_dynamic-update-slice_fusion.4
  408.1 0.6 fusion.45
  408.7 1.4 bitcast_dynamic-update-slice_fusion.4
  410.1 19.7 %custom-call.14 = f32[2,128,128]{1,2,0:T(8,128)S(1)} custom-call(f32[2,128,128]{2,1,0:T(8,128)S(1)} %get-tuple-element.21), custom_call_target="InvertDiagBlocksLowerTriangular" | custom-call | tf_op jit(solution)/shard_map/triangular_solve/custom-call.0 | solution.py:22
  429.8 0.3 fusion.15
  430.3 0.3 fusion.12
  430.6 1.1 fusion.3
  431.9 140.5 %all-reduce.6.cloned.1.call-done = f32[256,256]{0,1:T(8,128)} async-done(((f32[256,256]{0,1:T(8,128)}), f32[256,256]{0,1:T(8,128)}) %all-reduce.6.cloned.1.call-update) | async-done | bytes 262160 | tf_op jit(solution)/shard_map/psum | solution.py:26
  572.4 1.1 copy.7
  573.5 1.0 fusion.1
  574.5 11.7 %cholesky.164 = f32[128,128]{1,0:T(8,128)S(1)} custom-call(f32[128,128]{1,0:T(8,128)S(1)} %cholesky.197), custom_call_target="Cholesky" | custom-call | tf_op jit(solution)/shard_map/jit(cholesky)/cholesky | solution.py:21
  586.3 9.8 %custom-call.15 = f32[1,128,128]{1,2,0:T(8,128)S(1)} custom-call(f32[1,128,128]{2,1,0:T(8,128)S(1)} %get-tuple-element.46), custom_call_target="InvertDiagBlocksLowerTriangular" | custom-call | tf_op jit(solution)/shard_map/jit(cholesky)/cholesky | solution.py:21
  596.6 11.7 %cholesky.181 = f32[128,128]{1,0:T(8,128)S(1)} custom-call(f32[128,128]{1,0:T(8,128)S(1)} %convolution_subtract_fusion.1), custom_call_target="Cholesky" | custom-call | tf_op jit(solution)/shard_map/jit(cholesky)/cholesky | solution.py:21
  608.3 0.6 compare_reduce_fusion.1
  609.0 0.7 compare_reduce_fusion
  611.1 4.3 while.5
  611.3 0.6 fusion.46
  611.9 1.4 bitcast_dynamic-update-slice_fusion.5
  613.4 0.6 fusion.46
  614.0 1.4 bitcast_dynamic-update-slice_fusion.5
  615.4 19.7 %custom-call.16 = f32[2,128,128]{1,2,0:T(8,128)S(1)} custom-call(f32[2,128,128]{2,1,0:T(8,128)S(1)} %get-tuple-element.22), custom_call_target="InvertDiagBlocksLowerTriangular" | custom-call | tf_op jit(solution)/shard_map/triangular_solve/custom-call.0 | solution.py:22
  635.1 0.3 fusion.9
  635.6 0.3 fusion.7
  635.9 0.7 maximum_multiply_fusion
  636.6 46.4 %all-gather.2.cloned.1.call-done = f32[4096,256]{0,1:T(8,128)} async-done(((f32[128,256]{0,1:T(8,128)}), f32[4096,256]{0,1:T(8,128)}) %all-gather.2.cloned.1.call-update) | async-done | bytes 4194320 | tf_op jit(solution)/shard_map/all_gather | solution.py:55
  683.0 5.6 copy.8
  (33 shorter events, 1.9 us)
Async XLA Ops:
  6.5 212.3 %reduce-scatter.2.cloned.1.call-start = ((), (), s32[]{:S(2)}) async-start(), calls=%async_computation.1 | async-start | bytes 4325376 | tf_op jit(solution)/shard_map/reduce_scatter | solution.py:39
  6.5 113.4 %copy-start = (bf16[2048,4096]{1,0:T(8,128)(2,1)S(1)}, bf16[2048,4096]{1,0:T(8,128)(2,1)}, u32[]{:S(2)}) copy-start(bf16[2048,4096]{1,0:T(8,128)(2,1)} %param.5) | copy-start | bytes 50331652
  24.1 47.9 %collective-permute-start = (f32[2048,256]{1,0:T(8,128)S(1)}, f32[2048,256]{1,0:T(8,128)S(1)}, u32[]{:S(2)}, u32[]{:S(2)}) collective-permute-start(f32[2048,256]{1,0:T(8,128)S(1)} %fusion.29), channel_id=1, source_target_pairs={{0,32},{32,0},{64,96},{96,64},{1,33},{33,1},{65,97},{97,65},{2,34}... | collective-permute-start | bytes 6291464 | tf_op jit(solution)/shard_map/ppermute | solution.py:33
  72.2 47.7 %collective-permute-start.1 = (f32[2048,256]{1,0:T(8,128)S(1)}, f32[2048,256]{1,0:T(8,128)S(1)}, u32[]{:S(2)}, u32[]{:S(2)}) collective-permute-start(f32[2048,256]{1,0:T(8,128)S(1)} %add.35), channel_id=1, source_target_pairs={{0,64},{32,96},{64,0},{96,32},{1,65},{33,97},{65,1},{97,33},{2,66}... | collective-permute-start | bytes 6291464 | tf_op jit(solution)/shard_map/ppermute | solution.py:33
  134.9 233.0 %all-reduce.4.cloned.1.call-start = ((), (), s32[]{:S(2)}) async-start(), calls=%async_computation.2 | async-start | bytes 524288 | tf_op jit(solution)/shard_map/psum | solution.py:26
  220.9 351.6 %all-reduce.6.cloned.1.call-start = ((), (), s32[]{:S(2)}) async-start(), calls=%async_computation.3 | async-start | bytes 524288 | tf_op jit(solution)/shard_map/psum | solution.py:26
  431.7 251.3 %all-gather.2.cloned.1.call-start = ((), (), s32[]{:S(2)}) async-start(), calls=%async_computation.4 | async-start | bytes 4325376 | tf_op jit(solution)/shard_map/all_gather | solution.py:55
Sparse Core Ops, SparseCore 0:
  135.1 83.7 reduce-scatter.1
  223.6 144.2 all-reduce.3
  431.8 140.5 all-reduce.5
  636.7 46.2 all-gather.1
